TPU v7x, 256 devices: a whole 4x4x8 slice. The times are simulated.
256 devices in a mesh: space: 16 (over z, core), tm: 16 (over x, y).
Axes of the slice: x: 4, y: 4, z: 8, core: 2. Of those that a mesh axis runs over, the one named last changes fastest.
Arguments:
- velocity: bfloat16 [3, 128, 128, 8192], P(None, 'tm', 'space'), may hold values from -12 to 12, as said below
- metrics: bfloat16 [5, 128, 8192], P(None, 'space'), may hold values from 0.25 to 2
- basis: bfloat16 [32, 3, 128, 8192], P(None, None, 'space'), may hold values from -0.0034179688 to 0.0034179688
Outputs:
- coefficients: float32 [128, 32], P('tm')
- rfactor: float32 [128, 8], P('tm')
- window: float32 [512, 32], P('tm')
Inputs may be any that keep to these rules, and one draw needn't show every extreme that they name: `velocity`: entries are real velocities of order one.
All inputs are finite; a program needn't handle non-finite values.
Results may differ from a plain program's by a relative error of at most 0.0029.
Values may be sent and summed in bfloat16 or wider, within the bound.
A program may use at most 192 MiB of HBM per device.

v0:
```python
import jax
import jax.numpy as jnp
from jax import lax
from jax.sharding import PartitionSpec as P

NZ = 64


def with_halo(block, sides, width):
    for axis, dim in sides:
        count = lax.axis_size(axis)
        forward = [(i, i + 1) for i in range(count - 1)]
        forward.append((count - 1, 0))
        backward = [(target, source) for source, target in forward]
        low = lax.ppermute(
            lax.slice_in_dim(block, block.shape[dim] - width, None, axis=dim), axis, forward
        )
        high = lax.ppermute(lax.slice_in_dim(block, 0, width, axis=dim), axis, backward)
        block = jnp.concatenate([low, block, high], axis=dim)
    return block


def entering(part, axis, combine, identity):
    place = lax.axis_index(axis)
    gathered = lax.all_gather(part, axis)
    state = jnp.zeros_like(part) + jnp.asarray(identity, part.dtype)

    def one(lap, state):
        return combine(state, lax.dynamic_index_in_dim(gathered, lap, 0, False))

    return lax.fori_loop(0, place, one, state)


def vorticity_of(padded, metrics):
    field = padded.astype(jnp.float32)
    coeffs = metrics.astype(jnp.float32)
    dxi = (field[:, :, 2:] - field[:, :, :-2]) * 0.5
    inner = field[:, :, 1:-1]
    width = inner.shape[-1]
    zeros = jnp.zeros(inner.shape[:-1] + (NZ,), jnp.float32)
    upper = jnp.concatenate([inner[..., NZ:], zeros], -1)
    lower = jnp.concatenate([zeros, inner[..., :-NZ]], -1)
    deta = (upper - lower) * 0.5
    column = jnp.arange(width, dtype=jnp.int32) % NZ
    plus = jnp.where(column == NZ - 1, jnp.roll(inner, NZ - 1, -1), jnp.roll(inner, -1, -1))
    minus = jnp.where(column == 0, jnp.roll(inner, -(NZ - 1), -1), jnp.roll(inner, 1, -1))
    dzeta = (plus - minus) * 0.5
    xi_x = coeffs[0][None]
    eta_x = coeffs[1][None]
    xi_y = coeffs[2][None]
    eta_y = coeffs[3][None]
    zeta_z = coeffs[4][None]

    def ddx(comp):
        return xi_x * dxi[comp] + eta_x * deta[comp]

    def ddy(comp):
        return xi_y * dxi[comp] + eta_y * deta[comp]

    def ddz(comp):
        return zeta_z * dzeta[comp]

    first = ddy(2) - ddz(1)
    second = ddz(0) - ddx(2)
    third = ddx(1) - ddy(0)
    return jnp.stack([first, second, third]).astype(jnp.bfloat16)


def upper_factor(gram):
    return jnp.linalg.cholesky(gram).T


def on_device(velocity, metrics, basis):
    snaps_here = velocity.shape[1]
    planes = velocity.shape[2]
    rows_total = 3.0 * planes * lax.axis_size("space") * velocity.shape[3]
    padded = with_halo(velocity, (("space", 2),), 1)
    vort = vorticity_of(padded, metrics)
    coeff_part = jnp.einsum("csxm,rcxm->sr", vort, basis, preferred_element_type=jnp.float32)
    gram_part = (
        jnp.einsum("csxm,ctxm->st", vort, vort, preferred_element_type=jnp.float32) / rows_total
    )
    coeff, gram = lax.psum((coeff_part, gram_part), "space")
    factor = upper_factor(gram)
    term = jnp.dot(coeff.T, coeff, precision=lax.Precision.HIGHEST) / snaps_here

    def combine(earlier, later):
        return earlier + later

    before = entering(term, "tm", combine, jnp.zeros_like(term))
    window = before + term
    return (coeff, factor, window)


def solution(mesh):
    return jax.shard_map(
        on_device,
        mesh=mesh,
        in_specs=(
            P(None, "tm", "space", None),
            P(None, "space", None),
            P(None, None, "space", None),
        ),
        out_specs=(P("tm", None), P("tm", None), P("tm", None)),
        check_vma=False,
    )
```

profile of v0, /device:TPU:6, one launch (start us, length us, event | category | flops | bytes accessed | tf_op | source)
XLA Modules:
  0.0 166.1 jit_solution(4372816823427168826)
XLA Ops:
  0.6 3.7 %copy.6 = bf16[3,8,8,8192]{3,1,2,0:T(8,128)(2,1)S(1)} copy(bf16[3,8,8,8192]{3,2,1,0:T(8,128)(2,1)} %param.5) | data formatting | bytes 6291456 | tf_op args[0]
  4.3 0.9 fusion.30
  5.3 0.0 collective-permute-start
  5.3 5.3 %collective-permute-start.1 = (bf16[3,8,1,8192]{3,1,2,0:T(8,128)(2,1)}, bf16[3,8,1,8192]{3,1,2,0:T(8,128)(2,1)}, u32[]{:S(2)}, u32[]{:S(2)}) collective-permute-start(bf16[3,8,1,8192]{3,1,2,0:T(8,128)(2,1)} %get-tuple-element.54), channel_id=1, source_target_pairs={{16,0},{32,16},{48,32},{64,48},{80,64},{96,80},{112,96},{128,112},... | collective-permute-start | bytes 1179656 | tf_op jit(solution)/shard_map/ppermute | solution.py:18
  10.6 0.0 copy-done.7
  10.6 0.1 convert_element_type.7
  10.7 1.1 slice_bitcast_fusion.2
  11.8 4.5 %collective-permute-done = bf16[3,8,1,8192]{3,1,2,0:T(8,128)(2,1)S(1)} collective-permute-done((bf16[3,8,1,8192]{3,1,2,0:T(8,128)(2,1)}, bf16[3,8,1,8192]{3,1,2,0:T(8,128)(2,1)S(1)}, u32[]{:S(2)}, u32[]{:S(2)}) %collective-permute-start) | collective-permute-done | bytes 393248 | tf_op jit(solution)/shard_map/ppermute | solution.py:15
  16.2 0.0 collective-permute-done.1
  16.2 4.4 %maximum_convert_fusion = f32[3,8,10,8192]{3,1,2,0:T(8,128)} fusion(bf16[3,8,1,8192]{3,1,2,0:T(8,128)(2,1)} %collective-permute-done.1, bf16[3,8,8,8192]{3,1,2,0:T(8,128)(2,1)S(1)} %copy.6, bf16[3,8,1,8192]{3,1,2,0:T(8,128)(2,1)S(1)} %collective-permute-done), kind=kLoop, calls=%fused_computation.10 | loop fusion | flops 5898240 | bytes 11796480 | tf_op jit(solution)/shard_map/convert_element_type | solution.py:35
  20.6 11.0 %fusion.27 = (f32[3,8,8,8191]{3,1,2,0:T(8,128)}, f32[3,8,8,8191]{3,1,2,0:T(8,128)}) fusion(f32[3,8,10,8192]{3,1,2,0:T(8,128)} %maximum_convert_fusion), kind=kLoop, calls=%fused_computation.56 | loop fusion | bytes 25162752 | tf_op jit(solution)/shard_map/jit(_roll_static)/slice | solution.py:46
  31.6 11.0 %fusion.28 = (f32[3,8,8,8129]{3,1,2,0:T(8,128)}, f32[3,8,8,8129]{3,1,2,0:T(8,128)}) fusion(f32[3,8,10,8192]{3,1,2,0:T(8,128)} %maximum_convert_fusion), kind=kLoop, calls=%fused_computation.57 | loop fusion | bytes 24972288 | tf_op jit(solution)/shard_map/jit(_roll_static)/slice | solution.py:46
  42.6 11.0 %fusion.29 = (f32[3,8,8,8128]{3,1,2,0:T(8,128)}, f32[3,8,8,8128]{3,1,2,0:T(8,128)}) fusion(f32[3,8,10,8192]{3,1,2,0:T(8,128)} %maximum_convert_fusion), kind=kLoop, calls=%fused_computation.58 | loop fusion | bytes 24969216 | tf_op jit(solution)/shard_map/slice | solution.py:41
  53.6 14.8 %fusion.2 = (f32[3,8,8,8192]{3,1,2,0:T(8,128)}, f32[3,8,8,8192]{3,1,2,0:T(8,128)}) fusion(f32[3,8,10,8192]{3,1,2,0:T(8,128)} %maximum_convert_fusion, f32[3,8,8,8128]{3,1,2,0:T(8,128)} %get-tuple-element.48, f32[3,8,8,8128]{3,1,2,0:T(8,128)} %get-tuple-element.47), kind=kLoop, calls=%fused_computation.4 | loop fusion | flops 6291456 | bytes 37650432 | tf_op jit(solution)/shard_map/mul | solution.py:37
  68.4 0.1 maximum_convert_fusion.1
  68.5 0.7 maximum_convert_fusion.2
  69.2 2.1 %copy-done = f32[3,8,8,8129]{3,1,2,0:T(8,128)S(1)} copy-done((f32[3,8,8,8129]{3,1,2,0:T(8,128)S(1)}, f32[3,8,8,8129]{3,1,2,0:T(8,128)}, u32[]{:S(2)}) %copy-start) | copy-done | bytes 6243096
  71.4 9.0 %fusion.4 = f32[3,8,8,8192]{3,1,2,0:T(8,128)} fusion(f32[3,8,8,8129]{3,1,2,0:T(8,128)S(1)} %copy-done.1, f32[3,8,8,63]{3,1,2,0:T(8,128)} %get-tuple-element.52, f32[3,8,8,1]{3,1,2,0:T(8,128)S(1)} %get-tuple-element.50, f32[3,8,8,8191]{3,1,2,0:T(8,128)} %get-tuple-element.44, f32[3,8,8,63]{3,1,2,0:T(8,128)S(1)} %get-tuple-element.51, ...), kind=kLoop, calls=%fused_computation.7 | loop fusion | flops 12582912 | bytes 31473664 | tf_op jit(solution)/shard_map/mul | solution.py:47
  80.4 7.3 %fusion.12 = (bf16[1,8,8,8192]{3,1,2,0:T(8,128)(2,1)S(1)}, bf16[1,8,8,8192]{3,1,2,0:T(8,128)(2,1)S(1)}, bf16[1,8,8,8192]{3,1,2,0:T(8,128)(2,1)S(1)}) fusion(f32[3,8,8,8192]{3,1,2,0:T(8,128)} %fusion.4, f32[3,8,8,8192]{3,1,2,0:T(8,128)} %get-tuple-element.63, f32[3,8,8,8192]{3,1,2,0:T(8,128)} %get-tuple-element.62, f32[8,8192]{1,0:T(8,128)S(1)} %copy-done.2, ...), kind=kLoop, calls=%fused_computation.25 | loop fusion | flops 10485760 | bytes 21233664 | tf_op jit(solution)/shard_map/convert
  87.7 2.3 %fusion.18 = f32[8,8]{0,1:T(8,128)S(1)} fusion(bf16[1,8,8,8192]{3,1,2,0:T(8,128)(2,1)S(1)} %get-tuple-element.42, bf16[1,8,8,8192]{3,1,2,0:T(8,128)(2,1)S(1)} %get-tuple-element.41, bf16[1,8,8,8192]{3,1,2,0:T(8,128)(2,1)S(1)} %get-tuple-element.40), kind=kOutput, calls=%fused_computation.30 | convolution fusion | flops 28311616 | bytes 3145984 | tf_op jit(solution)/shard_map/csxm,ctxm->st/dot_general | solution.py:81
  90.0 21.2 %fusion.15 = f32[8,32]{1,0:T(8,128)S(1)} fusion(bf16[32,3,8,8192]{3,2,1,0:T(8,128)(2,1)} %param.7, bf16[1,8,8,8192]{3,1,2,0:T(8,128)(2,1)S(1)} %get-tuple-element.42, bf16[1,8,8,8192]{3,1,2,0:T(8,128)(2,1)S(1)} %get-tuple-element.41, bf16[1,8,8,8192]{3,1,2,0:T(8,128)(2,1)S(1)} %get-tuple-element.40), kind=kOutput, calls=%fused_computation.29 | convolution fusion | flops 103809024 | bytes 15729664 | tf_op jit(solution)/shard_map/csxm,rcxm->sr/dot_general | solution.py:79
  111.1 27.1 %all-reduce.2 = (f32[8,32]{1,0:T(8,128)S(1)}, f32[8,8]{0,1:T(8,128)S(1)}) all-reduce(f32[8,32]{1,0:T(8,128)S(1)} %fusion.15, f32[8,8]{0,1:T(8,128)S(1)} %fusion.18), channel_id=1, replica_groups=mesh['space'=16,'tm'=16] {'space'}, use_global_device_ids=true, to_apply=%region_0.1 | all-reduce | flops 320 | bytes 2560 | tf_op jit(solution)/shard_map/psum | solution.py:83
  138.2 0.0 copy-start.8
  138.3 0.2 convolution_multiply_fusion
  138.5 23.7 %all-gather = f32[512,32]{1,0:T(8,128)S(1)} all-gather(f32[32,32]{1,0:T(8,128)S(1)} %convolution_multiply_fusion), channel_id=2, replica_groups=mesh['space'=16,'tm'=16] {'tm'}, dimensions={0}, use_global_device_ids=true | all-gather | bytes 69632 | tf_op jit(solution)/shard_map/all_gather | solution.py:25
  162.2 0.5 while.10
  162.7 0.6 add.60
  163.3 0.1 copy.11
  163.4 0.7 cholesky.18
  164.1 0.6 compare_reduce_fusion
  164.8 0.6 select_bitcast_fusion
  165.4 0.7 copy.12
  (36 shorter events, 0.2 us)
Async XLA Ops:
  0.6 9.9 %copy-start.7 = (bf16[5,8,8192]{2,1,0:T(8,128)(2,1)S(1)}, bf16[5,8,8192]{2,1,0:T(8,128)(2,1)}, u32[]{:S(2)}) copy-start(bf16[5,8,8192]{2,1,0:T(8,128)(2,1)} %param.6) | copy-start | bytes 1966084
  5.3 11.0 %collective-permute-start = (bf16[3,8,1,8192]{3,1,2,0:T(8,128)(2,1)}, bf16[3,8,1,8192]{3,1,2,0:T(8,128)(2,1)S(1)}, u32[]{:S(2)}, u32[]{:S(2)}) collective-permute-start(bf16[3,8,1,8192]{3,1,2,0:T(8,128)(2,1)} %get-tuple-element.53), channel_id=1, source_target_pairs={{0,16},{16,32},{32,48},{48,64},{64,80},{80,96},{96,112},{112,128},... | collective-permute-start | bytes 1179656 | tf_op jit(solution)/shard_map/ppermute | solution.py:15
  5.3 11.0 %collective-permute-start.1 = (bf16[3,8,1,8192]{3,1,2,0:T(8,128)(2,1)}, bf16[3,8,1,8192]{3,1,2,0:T(8,128)(2,1)}, u32[]{:S(2)}, u32[]{:S(2)}) collective-permute-start(bf16[3,8,1,8192]{3,1,2,0:T(8,128)(2,1)} %get-tuple-element.54), channel_id=1, source_target_pairs={{16,0},{32,16},{48,32},{64,48},{80,64},{96,80},{112,96},{128,112},... | collective-permute-start | bytes 1179656 | tf_op jit(solution)/shard_map/ppermute | solution.py:18
  42.6 26.6 %slice-start = ((s8[6291456]{0:T(1024)(128)(4,1)}), s8[2097152]{0:T(1024)(128)(4,1)S(1)}, s32[]{:S(2)}) async-start(s8[6291456]{0:T(1024)(128)(4,1)} %bitcast.31), calls=%async_computation | async-start | bytes 4194304
  53.6 15.6 %slice-start.1 = ((s8[6291456]{0:T(1024)(128)(4,1)}), s8[4194304]{0:T(1024)(128)(4,1)S(1)}, s32[]{:S(2)}) async-start(s8[6291456]{0:T(1024)(128)(4,1)} %bitcast.31), calls=%async_computation.1 | async-start | bytes 8388608
  53.6 15.6 %copy-start.1 = (f32[3,8,8,8129]{3,1,2,0:T(8,128)S(1)}, f32[3,8,8,8129]{3,1,2,0:T(8,128)}, u32[]{:S(2)}) copy-start(f32[3,8,8,8129]{3,1,2,0:T(8,128)} %get-tuple-element.46) | copy-start | bytes 18729220
  68.4 2.9 %copy-start = (f32[3,8,8,8129]{3,1,2,0:T(8,128)S(1)}, f32[3,8,8,8129]{3,1,2,0:T(8,128)}, u32[]{:S(2)}) copy-start(f32[3,8,8,8129]{3,1,2,0:T(8,128)} %get-tuple-element.45) | copy-start | bytes 18729220
  71.3 9.0 %copy-start.2 = (f32[8,8192]{1,0:T(8,128)S(1)}, f32[8,8192]{1,0:T(8,128)}, u32[]{:S(2)}) copy-start(f32[8,8192]{1,0:T(8,128)} %get-tuple-element.55) | copy-start | bytes 786436
  71.4 9.0 %copy-start.3 = (f32[8,8192]{1,0:T(8,128)S(1)}, f32[8,8192]{1,0:T(8,128)}, u32[]{:S(2)}) copy-start(f32[8,8192]{1,0:T(8,128)} %get-tuple-element.56) | copy-start | bytes 786436
  71.4 9.0 %copy-start.4 = (f32[8,8192]{1,0:T(8,128)S(1)}, f32[8,8192]{1,0:T(8,128)}, u32[]{:S(2)}) copy-start(f32[8,8192]{1,0:T(8,128)} %get-tuple-element.57) | copy-start | bytes 786436
  71.4 9.0 %copy-start.5 = (f32[8,8192]{1,0:T(8,128)S(1)}, f32[8,8192]{1,0:T(8,128)}, u32[]{:S(2)}) copy-start(f32[8,8192]{1,0:T(8,128)} %get-tuple-element.58) | copy-start | bytes 786436
  71.4 9.0 %copy-start.6 = (f32[8,8192]{1,0:T(8,128)S(1)}, f32[8,8192]{1,0:T(8,128)}, u32[]{:S(2)}) copy-start(f32[8,8192]{1,0:T(8,128)} %get-tuple-element.59) | copy-start | bytes 786436
  138.2 27.9 %copy-start.8 = (f32[8,32]{1,0:T(8,128)}, f32[8,32]{1,0:T(8,128)S(1)}, u32[]{:S(2)}) copy-start(f32[8,32]{1,0:T(8,128)S(1)} %get-tuple-element.38) | copy-start | bytes 3076
where the time goes:
time: 166 us
  blocking collectives  50.8 us (31%)
  local copies, waits for them, and re-layouts  41.6 us (25%)
  other arithmetic  39.1 us (24%)
  matrix products  23.7 us (14%)
  starting transfers between devices  5.3 us (3%)
  waiting for transfers between devices  4.47 us (3%)
    psum x1, blocking collectives, on_device(): coeff, gram = lax.psum((coeff_part, gram_part), 'space')  27.1 us
    all_gather x1, blocking collectives, entering(): gathered = lax.all_gather(part, axis)  23.7 us
    dot_general x1, matrix products, on_device(): jnp.einsum('csxm,rcxm->sr', vort, basis, preferred_element_type=jnp.float32)  21.2 us
    mul x1, other arithmetic, vorticity_of(): dxi = (field[:, :, 2:] - field[:, :, :-2]) * 0.5  14.8 us
    slice x1, local copies, waits for them, and re-layouts, vorticity_of(): jnp.roll(inner, -(NZ - 1), -1)  11 us
    slice x1, local copies, waits for them, and re-layouts, vorticity_of(): jnp.roll(inner, 1, -1)  11 us
    slice x1, local copies, waits for them, and re-layouts, vorticity_of(): upper = jnp.concatenate([inner[..., NZ:], zeros], -1)  11 us
    mul x1, other arithmetic, vorticity_of(): dzeta = (plus - minus) * 0.5  8.99 us
  transfers between devices with their start and end apart: 2, of which 1 were waited for; matrix products, arithmetic and copies ran while one was open for 1% of the time, Pallas kernels for 0%

commit v1 on v0

v1 whole, which is shorter than its diff:
```python
import functools

import jax
import jax.numpy as jnp
from jax import lax
from jax.experimental import pallas as pl
from jax.experimental.pallas import tpu as pltpu
from jax.sharding import PartitionSpec as P

NZ = 64
LANES = 128
CHUNK = 1024
HIGH = lax.Precision.HIGHEST
MESH = pl.DeviceIdType.MESH
F32 = jnp.float32
BF16 = jnp.bfloat16


def iota(shape, dim):
    return lax.broadcasted_iota(jnp.int32, shape, dim)


def kernel(n_sp, n_tm, snaps, rank, planes, rows_total,
           vel_hbm, met_hbm, bas_hbm,
           coef_ref, rfac_ref, win_ref,
           vel, met, bas, metf, out_lo, out_hi, in_lo, in_hi, half_lo, half_hi,
           vort, acc_b, acc_v, part, call,
           sem_v, sem_m, sem_b, sem_slo, sem_shi, sem_rlo, sem_rhi,
           sem_ps, sem_pr, sem_cs, sem_cr):
    sp = lax.axis_index("space")
    tm = lax.axis_index("tm")
    cells = met_hbm.shape[2]
    chunks = cells // CHUNK
    tiles = CHUNK // LANES
    rows = snaps * planes
    brows = rank * planes
    right = lax.rem(sp + 1, n_sp)
    left = lax.rem(sp + n_sp - 1, n_sp)

    barrier = pltpu.get_barrier_semaphore()

    def hello_sp(d, _):
        pl.semaphore_signal(barrier, inc=1, device_id=(lax.rem(sp + d, n_sp), tm), device_id_type=MESH)
        return 0

    def hello_tm(d, _):
        pl.semaphore_signal(barrier, inc=1, device_id=(sp, lax.rem(tm + d, n_tm)), device_id_type=MESH)
        return 0

    lax.fori_loop(1, n_sp, hello_sp, 0)
    lax.fori_loop(1, n_tm, hello_tm, 0)

    def at(k):
        return pl.ds(pl.multiple_of(k * CHUNK, CHUNK), CHUNK)

    def vel_at(k):
        return pl.ds(pl.multiple_of(k * CHUNK + LANES, LANES), CHUNK)

    def vel_copy(k):
        return pltpu.make_async_copy(vel_hbm.at[:, at(k)], vel.at[:, vel_at(k)], sem_v.at[k])

    def bas_copy(k):
        return pltpu.make_async_copy(bas_hbm.at[:, :, :, at(k)], bas.at[:, :, :, at(k)], sem_b.at[k])

    met_copy = pltpu.make_async_copy(met_hbm, met, sem_m)

    def start_vel(k, _):
        vel_copy(k).start()
        return 0

    def start_bas(k, _):
        bas_copy(k).start()
        return 0

    lax.fori_loop(0, chunks, start_vel, 0)
    met_copy.start()
    lax.fori_loop(0, chunks, start_bas, 0)

    zero_tile = jnp.zeros((vel.shape[0], LANES), BF16)
    vel[:, pl.ds(0, LANES)] = zero_tile
    vel[:, pl.ds(cells + LANES, LANES)] = zero_tile
    acc_b[...] = jnp.zeros_like(acc_b)
    acc_v[...] = jnp.zeros_like(acc_v)

    edge = 3 * snaps
    pick_row = iota((2 * edge, vel.shape[0]), 0)
    pick_col = iota((2 * edge, vel.shape[0]), 1)
    wanted = jnp.where(pick_row < edge, pick_row * planes, (pick_row - edge) * planes + planes - 1)
    pick = jnp.where(pick_col == wanted, 1.0, 0.0).astype(BF16)

    def lo_copy(k):
        return pltpu.make_async_remote_copy(
            src_ref=out_lo.at[:, at(k)], dst_ref=in_hi.at[:, at(k)],
            send_sem=sem_slo.at[k], recv_sem=sem_rhi.at[k],
            device_id=(left, tm), device_id_type=MESH)

    def hi_copy(k):
        return pltpu.make_async_remote_copy(
            src_ref=out_hi.at[:, at(k)], dst_ref=in_lo.at[:, at(k)],
            send_sem=sem_shi.at[k], recv_sem=sem_rlo.at[k],
            device_id=(right, tm), device_id_type=MESH)

    def extract(k, _):
        vel_copy(k).wait()
        got = jnp.dot(pick, vel[:, vel_at(k)], preferred_element_type=F32).astype(BF16)
        out_lo[:, at(k)] = got[:edge]
        out_hi[:, at(k)] = got[edge:]
        return 0

    lax.fori_loop(0, chunks, extract, 0)
    pl.semaphore_wait(barrier, n_sp - 1 + n_tm - 1)

    def send(k, _):
        lo_copy(k).start()
        hi_copy(k).start()
        return 0

    lax.fori_loop(0, chunks, send, 0)
    met_copy.wait()
    for i in range(5):
        def scale(k, _):
            metf[i, :, at(k)] = met[i, :, at(k)].astype(F32) * 0.5
            return 0
        lax.fori_loop(0, chunks, scale, 0)

    lane = iota((planes, LANES), 1)
    row = iota((planes, LANES), 0)
    low_half = lane < NZ
    first_k = lane % NZ == 0
    last_k = lane % NZ == NZ - 1
    first_x = row == 0
    last_x = row == planes - 1

    def chunk(k, _):
        lo_copy(k).wait()
        hi_copy(k).wait()
        half_lo[...] = in_lo[:, at(k)].astype(F32)
        half_hi[...] = in_hi[:, at(k)].astype(F32)
        base = k * CHUNK

        def load(c, s, t):
            where = pl.ds(pl.multiple_of(base + (t + 1) * LANES, LANES), LANES)
            return vel[pl.ds((c * snaps + s) * planes, planes), where].astype(F32)

        for pair in range(snaps // 2):
            prev = {}
            cur = {}
            curR = {}
            D = {}
            for s in (2 * pair, 2 * pair + 1):
                for c in range(3):
                    a = pltpu.roll(load(c, s, -1), NZ, 1)
                    cur[s, c] = load(c, s, 0)
                    curR[s, c] = pltpu.roll(cur[s, c], NZ, 1)
                    D[s, c] = curR[s, c] - a
            for t in range(tiles):
                mwhere = pl.ds(pl.multiple_of(base + t * LANES, LANES), LANES)
                xi_x, eta_x, xi_y, eta_y, zeta = (metf[i, :, mwhere] for i in range(5))
                res = []
                for s in (2 * pair, 2 * pair + 1):
                    dxi, deta, dz = [], [], []
                    for c in range(3):
                        f = cur[s, c]
                        R = curR[s, c]
                        nxt = load(c, s, t + 1)
                        nxtR = pltpu.roll(nxt, NZ, 1)
                        Dn = nxtR - R
                        deta.append(jnp.where(low_half, D[s, c], Dn))
                        if c < 2:
                            plus = pltpu.roll(jnp.where(first_k, R, f), LANES - 1, 1)
                            minus = pltpu.roll(jnp.where(last_k, R, f), 1, 1)
                            dz.append(plus - minus)
                        lo = jnp.broadcast_to(half_lo[pl.ds(c * snaps + s, 1), pl.ds(t * LANES, LANES)], (planes, LANES))
                        hi = jnp.broadcast_to(half_hi[pl.ds(c * snaps + s, 1), pl.ds(t * LANES, LANES)], (planes, LANES))
                        xp = pltpu.roll(jnp.where(first_x, hi, f), planes - 1, 0)
                        xm = pltpu.roll(jnp.where(last_x, lo, f), 1, 0)
                        dxi.append(xp - xm)
                        cur[s, c], curR[s, c], D[s, c] = nxt, nxtR, Dn
                    one = xi_y * dxi[2] + eta_y * deta[2] - zeta * dz[1]
                    two = zeta * dz[0] - (xi_x * dxi[2] + eta_x * deta[2])
                    three = (xi_x * dxi[1] + eta_x * deta[1]) - (xi_y * dxi[0] + eta_y * deta[0])
                    res.append((one, two, three))
                for c in range(3):
                    both = jnp.concatenate([res[0][c], res[1][c]], axis=0).astype(BF16)
                    vort[c, pl.ds(2 * pair * planes, 2 * planes), pl.ds(t * LANES, LANES)] = both
        bas_copy(k).wait()
        nt = (((1,), (1,)), ((), ()))
        for c in range(3):
            v = vort[c]
            b = bas[:, c, :, at(k)].reshape(brows, CHUNK)
            acc_b[...] += lax.dot_general(v, b, nt, preferred_element_type=F32)
            acc_v[...] += lax.dot_general(v, v, nt, preferred_element_type=F32)
        return 0

    lax.fori_loop(0, chunks, chunk, 0)

    def keep_same(acc):
        same = iota(acc.shape, 0) % planes == iota(acc.shape, 1) % planes
        return jnp.where(same, acc[...], 0.0)

    def gather_to(count, first):
        src = iota((count, LANES), 0) // planes + first
        return jnp.where(src == iota((count, LANES), 1), 1.0, 0.0)

    wide = (jnp.dot(keep_same(acc_b), gather_to(brows, 0), preferred_element_type=F32, precision=HIGH)
            + jnp.dot(keep_same(acc_v), gather_to(rows, rank), preferred_element_type=F32, precision=HIGH))
    part[sp] = jnp.sum(wide.reshape(snaps, planes, LANES), axis=1)

    def part_copy(d):
        return pltpu.make_async_remote_copy(
            src_ref=part.at[sp], dst_ref=part.at[sp],
            send_sem=sem_ps.at[d], recv_sem=sem_pr.at[sp],
            device_id=(lax.rem(sp + d, n_sp), tm), device_id_type=MESH)

    def part_arrival(d):
        src = lax.rem(sp + d, n_sp)
        return pltpu.make_async_remote_copy(
            src_ref=part.at[src], dst_ref=part.at[src],
            send_sem=sem_ps.at[d], recv_sem=sem_pr.at[src],
            device_id=(src, tm), device_id_type=MESH)

    def part_start(d, _):
        part_copy(d).start()
        return 0

    def part_wait(d, _):
        part_arrival(d).wait_recv()
        return 0

    lax.fori_loop(1, n_sp, part_start, 0)
    lax.fori_loop(1, n_sp, part_wait, 0)
    total = jnp.sum(part[...], axis=0)
    wlane = iota((snaps, LANES), 1)
    call[tm] = jnp.where(wlane < rank, total, 0.0)

    def call_copy(d):
        return pltpu.make_async_remote_copy(
            src_ref=call.at[tm], dst_ref=call.at[tm],
            send_sem=sem_cs.at[d], recv_sem=sem_cr.at[tm],
            device_id=(sp, lax.rem(tm + d, n_tm)), device_id_type=MESH)

    def call_arrival(d):
        src = lax.rem(tm + d, n_tm)
        return pltpu.make_async_remote_copy(
            src_ref=call.at[src], dst_ref=call.at[src],
            send_sem=sem_cs.at[d], recv_sem=sem_cr.at[src],
            device_id=(sp, src), device_id_type=MESH)

    def call_start(d, _):
        call_copy(d).start()
        return 0

    def call_wait(d, _):
        call_arrival(d).wait_recv()
        return 0

    lax.fori_loop(1, n_tm, call_start, 0)

    coef_ref[...] = total[:, :rank]
    left_edge = pltpu.roll(total, LANES - rank, 1)
    a = jnp.where(wlane < snaps, left_edge, 0.0) / rows_total
    u_rows = []
    for j in range(snaps):
        d = a[j:j + 1, j:j + 1]
        line = a[j:j + 1, :]
        u_rows.append(jnp.where(iota((1, LANES), 1) >= j, line * lax.rsqrt(d), 0.0))
        if j < snaps - 1:
            a = a - (a[:, j:j + 1] / d) * line
    rfac_ref[...] = jnp.concatenate(u_rows, axis=0)[:, :snaps]

    lax.fori_loop(1, n_tm, call_wait, 0)
    every = call[...].reshape(n_tm * snaps, LANES)
    every = jnp.where(iota(every.shape, 0) < (tm + 1) * snaps, every, 0.0)
    win = lax.dot_general(every, every, (((0,), (0,)), ((), ())), preferred_element_type=F32, precision=HIGH)
    win_ref[...] = win[:rank, :rank] / snaps

    def part_end(d, _):
        part_copy(d).wait_send()
        return 0

    def call_end(d, _):
        call_copy(d).wait_send()
        return 0

    lax.fori_loop(1, n_sp, part_end, 0)
    lax.fori_loop(1, n_tm, call_end, 0)


def on_device(velocity, metrics, basis):
    n_sp = lax.axis_size("space")
    n_tm = lax.axis_size("tm")
    comps, snaps, planes, cells = velocity.shape
    rank = basis.shape[0]
    rows_total = float(3 * planes * n_sp * cells)
    chunks = cells // CHUNK
    vrows = comps * snaps * planes
    edge = comps * snaps
    anywhere = pl.BlockSpec(memory_space=pl.ANY)
    inside = pl.BlockSpec(memory_space=pltpu.VMEM)
    dma = pltpu.SemaphoreType.DMA
    return pl.pallas_call(
        functools.partial(kernel, n_sp, n_tm, snaps, rank, planes, rows_total),
        out_shape=(
            jax.ShapeDtypeStruct((snaps, rank), F32),
            jax.ShapeDtypeStruct((snaps, snaps), F32),
            jax.ShapeDtypeStruct((rank, rank), F32),
        ),
        in_specs=[anywhere] * 3,
        out_specs=(inside,) * 3,
        scratch_shapes=[
            pltpu.VMEM((vrows, cells + 2 * LANES), BF16),
            pltpu.VMEM(metrics.shape, BF16),
            pltpu.VMEM(basis.shape, BF16),
            pltpu.VMEM(metrics.shape, F32),
            pltpu.VMEM((edge, cells), BF16),
            pltpu.VMEM((edge, cells), BF16),
            pltpu.VMEM((edge, cells), BF16),
            pltpu.VMEM((edge, cells), BF16),
            pltpu.VMEM((edge, CHUNK), F32),
            pltpu.VMEM((edge, CHUNK), F32),
            pltpu.VMEM((comps, snaps * planes, CHUNK), BF16),
            pltpu.VMEM((snaps * planes, rank * planes), F32),
            pltpu.VMEM((snaps * planes, snaps * planes), F32),
            pltpu.VMEM((n_sp, snaps, LANES), F32),
            pltpu.VMEM((n_tm, snaps, LANES), F32),
            dma((chunks,)), dma(()), dma((chunks,)),
            dma((chunks,)), dma((chunks,)), dma((chunks,)), dma((chunks,)),
            dma((n_sp,)), dma((n_sp,)), dma((n_tm,)), dma((n_tm,)),
        ],
        compiler_params=pltpu.CompilerParams(collective_id=0, has_side_effects=True),
    )(velocity.reshape(vrows, cells), metrics, basis)


def solution(mesh):
    return jax.shard_map(
        on_device,
        mesh=mesh,
        in_specs=(
            P(None, "tm", "space", None),
            P(None, "space", None),
            P(None, None, "space", None),
        ),
        out_specs=(P("tm", None), P("tm", None), P("tm", None)),
        check_vma=False,
    )
```

time: 166 us -> 49.4 us (0.30)
  the two profiles are of different devices: /device:TPU:6 before, /device:TPU:1 now
where the time goes in v1:
time: 49.4 us; the launch traced here: 49.2 us
  Pallas kernels  44.7 us (90%)
  local copies, waits for them, and re-layouts  3.86 us (8%)
  between operations  0.64 us (1%)
    pallas_call x1, Pallas kernels, on_device(): pl.pallas_call(functools.partial(kernel, n_sp, n_tm, snaps, rank, planes,...  44.7 us
    unnamed x3, local copies, waits for them, and re-layouts  3.86 us

profile of v1, /device:TPU:1, one launch (start us, length us, event | category | flops | bytes accessed | tf_op | source)
XLA Modules:
  0.0 49.2 jit_solution(17197857032840687903)
XLA Ops:
  0.6 44.7 %shard_map.58 = (f32[8,32]{1,0:T(8,128)}, f32[8,8]{1,0:T(8,128)}, f32[32,32]{1,0:T(8,128)}) custom-call(bf16[192,8192]{1,0:T(8,128)(2,1)} %bitcast.1, bf16[5,8,8192]{2,1,0:T(8,128)(2,1)} %met_hbm.1, bf16[32,3,8,8192]{3,2,1,0:T(8,128)(2,1)} %bas_hbm.1), custom_call_target="tpu_custom_call" | custom-call | tf_op jit(solution)/shard_map/pallas_call | solution.py:301
  45.3 1.3 %copy.9 = f32[8,32]{1,0:T(8,128)} copy(f32[8,32]{1,0:T(8,128)} %get-tuple-element.6) | data formatting | bytes 2048
  46.6 1.3 %copy.10 = f32[8,8]{1,0:T(8,128)} copy(f32[8,8]{1,0:T(8,128)} %get-tuple-element.7) | data formatting | bytes 512
  47.8 1.3 %copy.11 = f32[32,32]{1,0:T(8,128)} copy(f32[32,32]{1,0:T(8,128)} %get-tuple-element.8) | data formatting | bytes 8192
